TPU v7x, 32 devices: a whole 2x2x4 slice. The times are simulated.
32 devices in a mesh: groups: 2 (over y), block: 4 (over x, core), tensor: 4 (over z).
Axes of the slice: x: 2, y: 2, z: 4, core: 2. Of those that a mesh axis runs over, the one named last changes fastest.
Arguments:
- tokens: bfloat16 [4096, 5120], P(('groups', 'block', 'tensor')), parts along dimension 0, may hold values from -20 to 20
- mod_shift: float32 [5120], replicated, may hold values from -3 to 3
- mod_scale: float32 [5120], replicated, may hold values from -0.5 to 0.5
- w_qkv: bfloat16 [3, 5120, 1024], P(None, 'block', 'tensor'), may hold values from -1 to 1
- tile_list: int32 [8, 4, 5], P(('groups', 'block')), parts along dimension 0, may hold values from 0 to 7, as said below
- tile_count: int32 [8, 4], P(('groups', 'block')), parts along dimension 0, may hold values from 2 to 5, as said below
Outputs:
- attended: bfloat16 [4096, 1024], P(('groups', 'block'), 'tensor'), parts along dimension 0
There are 2 independent parts, one for each index of `groups`. A program takes and returns all parts, laid end to end along the dimension named above; an argument that names none is the same for every part. Nothing has to cross between parts.
Inputs may be any that keep to these rules, and one draw needn't show every extreme that they name: `tile_list`: within the first tile_count[c, t] slots the entries are distinct, the first is the query tile itself (2 + t), and none names a tile outside the slab; blocks at scene cuts name no tile of the block across the cut. Later slots hold indices in range and are not read. `tile_count`: the first query tile of every block reads 5 slots.
All inputs are finite; a program needn't handle non-finite values.
Results may differ from a plain program's by a relative error of at most 0.0087.
Values may be sent and summed in bfloat16 or wider, within the bound.
No kernel may reach another device: no remote copies, remote signals or barrier semaphores. Data moves between devices by JAX's collectives and lax.ppermute only.
A program may use at most 64 MiB of HBM per device.

v0:
```python
import jax
import jax.numpy as jnp
from jax import lax
from jax.sharding import PartitionSpec as P

HEAD_DIM = 128
TILE = 128
BT = 2
epsilon = 1e-06


def with_halo(x, sides, width):
    for axis, dim in sides:
        count, length = (lax.axis_size(axis), x.shape[dim])
        up = [(i, (i + 1) % count) for i in range(count - 1)]
        down = [(j, i) for i, j in up]
        last = lax.slice_in_dim(x, length - width, length, axis=dim)
        first = lax.slice_in_dim(x, 0, width, axis=dim)
        before = lax.ppermute(last, axis, up)
        after = lax.ppermute(first, axis, down)
        x = jnp.concatenate([before, x, after], axis=dim)
    return x


def attend(queries, key_rows, value_rows, chosen_list, chosen_count):
    head_count = queries.shape[1] // HEAD_DIM
    local_tiles = queries.shape[0] // TILE
    all_tiles = key_rows.shape[0] // TILE
    slot_count = chosen_list.shape[1]
    shaped_queries = queries.reshape(local_tiles, TILE, head_count, HEAD_DIM)
    key_tiles = key_rows.reshape(all_tiles, TILE, head_count, HEAD_DIM)[chosen_list]
    value_tiles = value_rows.reshape(all_tiles, TILE, head_count, HEAD_DIM)[chosen_list]
    scores = jnp.einsum(
        "pthd,pkshd->phtks", shaped_queries, key_tiles, preferred_element_type=jnp.float32
    )
    scores = scores * HEAD_DIM ** (-0.5)
    live_slot = jnp.arange(slot_count, dtype=jnp.int32)[None, :] < chosen_count[:, None]
    scores = jnp.where(live_slot[:, None, None, :, None], scores, jnp.float32(-1e30))
    highest = jnp.max(scores, axis=(3, 4), keepdims=True)
    exponent = jnp.exp(scores - highest)
    denominator = jnp.sum(exponent, axis=(3, 4), keepdims=True)
    attn_weights = (exponent / denominator).astype(jnp.bfloat16)
    mixed = jnp.einsum(
        "phtks,pkshd->pthd", attn_weights, value_tiles, preferred_element_type=jnp.float32
    )
    return mixed.astype(jnp.bfloat16).reshape(local_tiles * TILE, head_count * HEAD_DIM)


def shards(tokens, mod_shift, mod_scale, w_qkv, tile_list, tile_count):
    values_in = tokens.astype(jnp.float32)
    row_mean = jnp.mean(values_in, axis=1, keepdims=True)
    centred = values_in - row_mean
    row_var = jnp.mean(centred * centred, axis=1, keepdims=True)
    normed = (centred * lax.rsqrt(row_var + epsilon) * (1.0 + mod_scale) + mod_shift).astype(
        jnp.bfloat16
    )
    gathered = lax.all_gather(normed, "tensor", axis=0, tiled=True)
    projected = jnp.einsum(
        "td,ide->ite",
        gathered,
        lax.all_gather(w_qkv, "block", axis=1, tiled=True),
        preferred_element_type=jnp.float32,
    )
    projected = projected.astype(jnp.bfloat16)
    queries = projected[0]
    key_value = projected[1:3]
    extended = with_halo(key_value, (("block", 1),), BT * TILE)
    return attend(queries, extended[0], extended[1], tile_list[0], tile_count[0])


def solution(mesh):
    return jax.shard_map(
        shards,
        mesh=mesh,
        in_specs=(
            P(("groups", "block", "tensor"), None),
            P(),
            P(),
            P(None, "block", "tensor"),
            P(("groups", "block"), None, None),
            P(("groups", "block"), None),
        ),
        out_specs=P(("groups", "block"), "tensor"),
        check_vma=False,
    )
```

profile of v0, /device:TPU:1, one launch (start us, length us, event | category | flops | bytes accessed | tf_op | source)
XLA Modules:
  0.0 203.5 jit_solution(6897856617463823574)
XLA Ops:
  6.5 0.0 copy-start
  6.5 0.0 copy-start.2
  6.5 0.0 copy-start.1
  6.5 0.0 all-gather.3.cloned.1.call-start
  6.5 1.7 convert_reduce_fusion
  8.2 1.8 fusion.4
  10.1 0.0 copy-done.2
  10.1 0.0 copy-done
  10.1 0.0 copy-done.1
  10.1 0.0 copy-start.3
  10.1 1.7 fusion.7
  11.8 0.0 all-gather.3.cloned.1.call-update
  11.8 0.0 all-gather.5.cloned.1.call-start
  11.9 0.7 all-gather.5.cloned.1.call-update
  12.6 0.0 copy-done.3
  12.6 0.1 reshape.73
  12.7 0.0 copy-start.4
  12.7 99.4 %all-gather.3.cloned.1.call-done = bf16[512,5120]{1,0:T(8,128)(2,1)} async-done(((bf16[128,5120]{1,0:T(8,128)(2,1)}), bf16[512,5120]{1,0:T(8,128)(2,1)}) %all-gather.3.cloned.1.call-update) | async-done | bytes 5242896 | tf_op jit(solution)/shard_map/all_gather | solution.py:57
  112.1 55.6 %all-gather.5.cloned.1.call-done = bf16[3,5120,256]{2,1,0:T(8,128)(2,1)} async-done(((bf16[3,1280,256]{2,1,0:T(8,128)(2,1)}), bf16[3,5120,256]{2,1,0:T(8,128)(2,1)}) %all-gather.5.cloned.1.call-update) | async-done | bytes 7864336 | tf_op jit(solution)/shard_map/all_gather | solution.py:61
  167.7 9.0 %fusion.16 = bf16[3,512,256]{2,1,0:T(8,128)(2,1)S(1)} fusion(bf16[3,5120,256]{2,1,0:T(8,128)(2,1)} %all-gather.5.cloned.1.call-done, bf16[512,5120]{1,0:T(8,128)(2,1)} %all-gather.3.cloned.1.call-done), kind=kOutput, calls=%fused_computation.21 | convolution fusion | flops 4026925056 | bytes 13893632 | tf_op jit(solution)/shard_map/td,ide->ite/dot_general | solution.py:58
  176.7 2.1 %collective-permute-start = (bf16[2,256,256]{2,1,0:T(8,128)(2,1)S(1)}, bf16[2,256,256]{2,1,0:T(8,128)(2,1)S(1)}, u32[]{:S(2)}, u32[]{:S(2)}) collective-permute-start(bf16[2,256,256]{2,1,0:T(8,128)(2,1)S(1)} %get-tuple-element.7), channel_id=1, source_target_pairs={{0,4},{4,8},{8,12},{1,5},{5,9},{9,13},{2,6},{6,10},{10,14},{3,7},{... | collective-permute-start | bytes 786440 | tf_op jit(solution)/shard_map/ppermute | solution.py:19
  178.9 2.2 %collective-permute-start.1 = (bf16[2,256,256]{2,1,0:T(8,128)(2,1)S(1)}, bf16[2,256,256]{2,1,0:T(8,128)(2,1)S(1)}, u32[]{:S(2)}, u32[]{:S(2)}) collective-permute-start(bf16[2,256,256]{2,1,0:T(8,128)(2,1)S(1)} %get-tuple-element.8), channel_id=1, source_target_pairs={{4,0},{8,4},{12,8},{5,1},{9,5},{13,9},{6,2},{10,6},{14,10},{7,3},{... | collective-permute-start | bytes 786440 | tf_op jit(solution)/shard_map/ppermute | solution.py:20
  181.1 0.0 copy-done.4
  181.1 0.1 iota_compare_fusion
  181.3 0.1 reshape_squeeze.10
  181.3 0.8 collective-permute-done
  182.2 4.4 %collective-permute-done.1 = bf16[2,256,256]{2,1,0:T(8,128)(2,1)S(1)} collective-permute-done((bf16[2,256,256]{2,1,0:T(8,128)(2,1)S(1)}, bf16[2,256,256]{2,1,0:T(8,128)(2,1)S(1)}, u32[]{:S(2)}, u32[]{:S(2)}) %collective-permute-start.1) | collective-permute-done | bytes 262176 | tf_op jit(solution)/shard_map/ppermute | solution.py:20
  186.6 0.1 pad_maximum_fusion
  186.6 0.1 fusion.32
  186.7 0.1 reshape_squeeze.11
  186.9 0.1 copy.15
  187.0 0.8 gather_fusion.1
  187.8 0.1 copy.17
  187.9 0.5 fusion.28
  188.4 0.4 fusion.8
  188.8 0.6 fusion.9
  189.4 0.9 reshape_squeeze.9
  190.3 1.1 copy.14
  191.5 1.9 gather_fusion
  193.3 2.4 %fusion.25 = bf16[4,128,2,128]{1,3,2,0:T(8,128)(2,1)S(1)} fusion(f32[4,2,128,5,128]{2,4,3,1,0:T(8,128)S(1)} %bitcast.38, f32[4,2,128]{2,1,0:T(2,128)S(1)} %fusion.9, f32[4,2,128]{2,1,0:T(2,128)S(1)} %fusion.8, pred[4,5]{1,0:T(4,128)(4,1)S(1)} %iota_compare_fusion, bf16[4,5,128,2,128]{4,2,3,1,0:T(8,128)(2,1)} %bitcast.41), kind=kOutput, calls=%fused_computation.24 | convolution fusion | flops 171180032 | bytes 4202516 | tf_op jit(solution)/shard_map/phtks,pkshd->pthd/dot_general | solution.py:43
  195.8 0.2 copy.20
  195.9 0.7 copy.37
  (8 shorter events, 0.1 us)
Async XLA Ops:
  6.5 3.6 %copy-start = (bf16[128,5120]{1,0:T(8,128)(2,1)S(1)}, bf16[128,5120]{1,0:T(8,128)(2,1)}, u32[]{:S(2)}) copy-start(bf16[128,5120]{1,0:T(8,128)(2,1)} %param.6) | copy-start | bytes 3932164
  6.5 3.5 %copy-start.2 = (f32[5120]{0:T(1024)S(1)}, f32[5120]{0:T(1024)}, u32[]{:S(2)}) copy-start(f32[5120]{0:T(1024)} %param.8) | copy-start | bytes 61444
  6.5 3.6 %copy-start.1 = (f32[5120]{0:T(1024)S(1)}, f32[5120]{0:T(1024)}, u32[]{:S(2)}) copy-start(f32[5120]{0:T(1024)} %param.7) | copy-start | bytes 61444
  6.5 105.5 %all-gather.3.cloned.1.call-start = ((), (), s32[]{:S(2)}) async-start(), calls=%async_computation | async-start | bytes 6553600 | tf_op jit(solution)/shard_map/all_gather | solution.py:57
  10.1 2.4 %copy-start.3 = (s32[1,4,5]{2,1,0:T(4,128)S(1)}, s32[1,4,5]{2,1,0:T(4,128)}, u32[]{:S(2)}) copy-start(s32[1,4,5]{2,1,0:T(4,128)} %param.10) | copy-start | bytes 244
  11.8 155.9 %all-gather.5.cloned.1.call-start = ((), (), s32[]{:S(2)}) async-start(), calls=%async_computation.1 | async-start | bytes 9830400 | tf_op jit(solution)/shard_map/all_gather | solution.py:61
  12.7 168.5 %copy-start.4 = (s32[1,4]{1,0:T(1,128)S(1)}, s32[1,4]{1,0:T(1,128)}, u32[]{:S(2)}) copy-start(s32[1,4]{1,0:T(1,128)} %param.11) | copy-start | bytes 52
  176.7 5.4 %collective-permute-start = (bf16[2,256,256]{2,1,0:T(8,128)(2,1)S(1)}, bf16[2,256,256]{2,1,0:T(8,128)(2,1)S(1)}, u32[]{:S(2)}, u32[]{:S(2)}) collective-permute-start(bf16[2,256,256]{2,1,0:T(8,128)(2,1)S(1)} %get-tuple-element.7), channel_id=1, source_target_pairs={{0,4},{4,8},{8,12},{1,5},{5,9},{9,13},{2,6},{6,10},{10,14},{3,7},{... | collective-permute-start | bytes 786440 | tf_op jit(solution)/shard_map/ppermute | solution.py:19
  178.9 7.7 %collective-permute-start.1 = (bf16[2,256,256]{2,1,0:T(8,128)(2,1)S(1)}, bf16[2,256,256]{2,1,0:T(8,128)(2,1)S(1)}, u32[]{:S(2)}, u32[]{:S(2)}) collective-permute-start(bf16[2,256,256]{2,1,0:T(8,128)(2,1)S(1)} %get-tuple-element.8), channel_id=1, source_target_pairs={{4,0},{8,4},{12,8},{5,1},{9,5},{13,9},{6,2},{10,6},{14,10},{7,3},{... | collective-permute-start | bytes 786440 | tf_op jit(solution)/shard_map/ppermute | solution.py:20
Sparse Core Ops, SparseCore 0:
  11.9 100.1 all-gather.2
  113.6 54.0 all-gather.4
where the time goes:
time: 204 us
  waiting for transfers between devices  161 us (79%)
  between operations  13.6 us (7%)
  matrix products  11.9 us (6%)
  other arithmetic  6.35 us (3%)
  local copies, waits for them, and re-layouts  6.3 us (3%)
  starting transfers between devices  4.38 us (2%)
    all_gather x1, waiting for transfers between devices, shards(): gathered = lax.all_gather(normed, 'tensor', axis=0, tiled=True)  99.4 us
    all_gather x1, waiting for transfers between devices, shards(): lax.all_gather(w_qkv, 'block', axis=1, tiled=True)  55.6 us
    dot_general x1, matrix products, shards(): jnp.einsum('td,ide->ite', gathered, lax.all_gather(w_qkv, 'block', axis=1...  9.01 us
    ppermute x1, waiting for transfers between devices, with_halo(): after = lax.ppermute(first, axis, down)  4.4 us
  transfers between devices with their start and end apart: 4, of which 4 were waited for; matrix products, arithmetic and copies ran while one was open for 0% of the time, Pallas kernels for 0%

commit v1 on v0

--- a/solution.py
+++ b/solution.py
@@ -54,7 +54,14 @@
     normed = (centred * lax.rsqrt(row_var + epsilon) * (1.0 + mod_scale) + mod_shift).astype(
         jnp.bfloat16
     )
-    gathered = lax.all_gather(normed, "tensor", axis=0, tiled=True)
+    size = lax.axis_size("tensor")
+    route = [(i_2, (i_2 + 1) % size) for i_2 in range(size)]
+    shards_2 = [normed]
+    for stride in range(1, size):
+        shards_2 = [lax.ppermute(shards_2[0], "tensor", route), *shards_2]
+    whole = jnp.concatenate(shards_2, axis=0)
+    offset = (lax.axis_index("tensor") + 1) * shards_2[-1].shape[0]
+    gathered = jnp.roll(whole, offset, axis=0)
     projected = jnp.einsum(
         "td,ide->ite",
         gathered,

time: 204 us -> 158 us (0.77)
  waiting for transfers between devices: 161 us -> 98 us
  local copies, waits for them, and re-layouts: 6.3 us -> 19.1 us
  starting transfers between devices: 4.38 us -> 9.62 us
    all_gather x1 -> x0, waiting for transfers between devices: 99.4 us -> none  [shards(): gathered = lax.all_gather(normed, 'tensor', axis=0, tiled=True)]
    ppermute x0 -> x3, waiting for transfers between devices: none -> 91.7 us  [shards(): shards_2 = [lax.ppermute(shards_2[0], 'tensor', route), *shards_2]]
    all_gather x1, waiting for transfers between devices: 55.6 us -> 0.01 us  [shards(): lax.all_gather(w_qkv, 'block', axis=1, tiled=True)]
    unnamed x11 -> x17, local copies, waits for them, and re-layouts: 0.76 us -> 13.6 us
    ppermute x1, starting transfers between devices: 2.12 us -> 5.53 us  [with_halo(): before = lax.ppermute(last, axis, up)]
    ppermute x0 -> x3, starting transfers between devices: none -> 2.17 us  [shards(): shards_2 = [lax.ppermute(shards_2[0], 'tensor', route), *shards_2]]
  transfers between devices with their start and end apart: 4 -> 6, of which waited for: 4 -> 5; matrix products, arithmetic and copies ran while one was open for 0% -> 11% of each run, Pallas kernels for 0% -> 0%
where the time goes in v1:
time: 158 us
  waiting for transfers between devices  98 us (62%)
  local copies, waits for them, and re-layouts  19.1 us (12%)
  between operations  13.6 us (9%)
  matrix products  11.9 us (8%)
  starting transfers between devices  9.62 us (6%)
  other arithmetic  5.78 us (4%)
    ppermute x3, waiting for transfers between devices, shards(): shards_2 = [lax.ppermute(shards_2[0], 'tensor', route), *shards_2]  91.7 us
    unnamed x17, local copies, waits for them, and re-layouts  13.6 us
    dot_general x1, matrix products, shards(): jnp.einsum('td,ide->ite', gathered, lax.all_gather(w_qkv, 'block', axis=1...  9.02 us
    ppermute x1, starting transfers between devices, with_halo(): before = lax.ppermute(last, axis, up)  5.53 us
    ppermute x1, waiting for transfers between devices, with_halo(): after = lax.ppermute(first, axis, down)  4.4 us
  transfers between devices with their start and end apart: 6, of which 5 were waited for; matrix products, arithmetic and copies ran while one was open for 11% of the time, Pallas kernels for 0%

profile of v1, /device:TPU:1, one launch (start us, length us, event | category | flops | bytes accessed | tf_op | source)
XLA Modules:
  0.0 158.0 jit_solution(14880943317701691915)
XLA Ops:
  6.5 0.0 copy-start
  6.5 0.0 copy-start.2
  6.5 0.0 copy-start.1
  6.5 0.0 all-gather.2.cloned.1.call-start
  6.5 0.7 all-gather.2.cloned.1.call-update
  7.3 0.6 copy-done
  7.9 0.0 copy-start.3
  7.9 0.3 convert_reduce_fusion
  8.1 0.5 fusion.5
  8.6 0.0 copy-done.2
  8.7 0.0 copy-done.1
  8.7 0.6 fusion.8
  9.3 2.2 %collective-permute-start = (bf16[128,5120]{1,0:T(8,128)(2,1)S(1)}, bf16[128,5120]{1,0:T(8,128)(2,1)S(1)}, u32[]{:S(2)}, u32[]{:S(2)}) collective-permute-start(bf16[128,5120]{1,0:T(8,128)(2,1)S(1)} %fusion.8), channel_id=1, source_target_pairs={{0,1},{1,2},{2,3},{3,0},{4,5},{5,6},{6,7},{7,4},{8,9},{9,10},{10,1... | collective-permute-start | bytes 3932168 | tf_op jit(solution)/shard_map/ppermute | solution.py:61
  11.4 30.5 %collective-permute-done = bf16[128,5120]{1,0:T(8,128)(2,1)S(1)} collective-permute-done((bf16[128,5120]{1,0:T(8,128)(2,1)S(1)}, bf16[128,5120]{1,0:T(8,128)(2,1)S(1)}, u32[]{:S(2)}, u32[]{:S(2)}) %collective-permute-start) | collective-permute-done | bytes 1310752 | tf_op jit(solution)/shard_map/ppermute | solution.py:61
  41.9 0.0 collective-permute-start.1
  41.9 31.0 %collective-permute-done.1 = bf16[128,5120]{1,0:T(8,128)(2,1)} collective-permute-done((bf16[128,5120]{1,0:T(8,128)(2,1)S(1)}, bf16[128,5120]{1,0:T(8,128)(2,1)}, u32[]{:S(2)}, u32[]{:S(2)}) %collective-permute-start.1) | collective-permute-done | bytes 1310752 | tf_op jit(solution)/shard_map/ppermute | solution.py:61
  72.9 0.0 collective-permute-start.2
  72.9 0.0 copy-done.3
  72.9 0.1 reshape.73
  73.0 30.2 %collective-permute-done.2 = bf16[128,5120]{1,0:T(8,128)(2,1)} collective-permute-done((bf16[128,5120]{1,0:T(8,128)(2,1)}, bf16[128,5120]{1,0:T(8,128)(2,1)}, u32[]{:S(2)}, u32[]{:S(2)}) %collective-permute-start.2) | collective-permute-done | bytes 1310752 | tf_op jit(solution)/shard_map/ppermute | solution.py:61
  103.3 2.5 %constant_dynamic-update-slice_fusion.7 = bf16[1024,5120]{1,0:T(8,128)(2,1)} fusion(bf16[128,5120]{1,0:T(8,128)(2,1)} %collective-permute-done.2), kind=kLoop, calls=%fused_computation.37 | loop fusion | bytes 2621440
  105.7 2.5 %constant_dynamic-update-slice_fusion.6 = bf16[1024,5120]{1,0:T(8,128)(2,1)} fusion(bf16[1024,5120]{1,0:T(8,128)(2,1)} %constant_dynamic-update-slice_fusion.7, bf16[128,5120]{1,0:T(8,128)(2,1)} %collective-permute-done.1), kind=kLoop, calls=%fused_computation.36 | loop fusion | bytes 2621440
  108.2 1.2 constant_dynamic-update-slice_fusion.5
  109.3 1.6 %constant_dynamic-update-slice_fusion.4 = bf16[1024,5120]{1,0:T(8,128)(2,1)} fusion(bf16[1024,5120]{1,0:T(8,128)(2,1)} %constant_dynamic-update-slice_fusion.5, f32[5120]{0:T(1024)S(1)} %copy-done.1, f32[5120]{0:T(1024)S(1)} %broadcast_add_fusion, f32[128]{0:T(128)S(1)} %add_rsqrt_fusion, f32[128]{0:T(128)S(1)} %broadcast_multiply_fusion, ...), kind=kLoop, calls=%fused_computation.34 | loop fusion | flops 3932160 | bytes 2663424
  111.0 2.5 %constant_dynamic-update-slice_fusion.3 = bf16[1024,5120]{1,0:T(8,128)(2,1)} fusion(bf16[1024,5120]{1,0:T(8,128)(2,1)} %constant_dynamic-update-slice_fusion.4, bf16[128,5120]{1,0:T(8,128)(2,1)} %collective-permute-done.2), kind=kLoop, calls=%fused_computation.33 | loop fusion | bytes 2621440
  113.5 2.5 %constant_dynamic-update-slice_fusion.2 = bf16[1024,5120]{1,0:T(8,128)(2,1)} fusion(bf16[1024,5120]{1,0:T(8,128)(2,1)} %constant_dynamic-update-slice_fusion.3, bf16[128,5120]{1,0:T(8,128)(2,1)} %collective-permute-done.1), kind=kLoop, calls=%fused_computation.32 | loop fusion | bytes 2621440
  115.9 1.2 constant_dynamic-update-slice_fusion.1
  117.2 1.6 %constant_dynamic-update-slice_fusion = bf16[1024,5120]{1,0:T(8,128)(2,1)} fusion(bf16[1024,5120]{1,0:T(8,128)(2,1)} %constant_dynamic-update-slice_fusion.1, f32[5120]{0:T(1024)S(1)} %copy-done.1, f32[5120]{0:T(1024)S(1)} %broadcast_add_fusion, f32[128]{0:T(128)S(1)} %add_rsqrt_fusion, f32[128]{0:T(128)S(1)} %broadcast_multiply_fusion, ...), kind=kLoop, calls=%fused_computation.30 | loop fusion | flops 3932160 | bytes 2663424 | tf_op jit(solution)/shard_map/jit(_roll_dynamic)/concatenate | solution.py:64
  118.8 0.0 copy-start.4
  118.8 0.0 all-gather.2.cloned.1.call-done
  118.8 9.0 %fusion.17 = bf16[3,512,256]{2,1,0:T(8,128)(2,1)S(1)} fusion(bf16[3,5120,256]{2,1,0:T(8,128)(2,1)} %all-gather.2.cloned.1.call-done, bf16[1024,5120]{1,0:T(8,128)(2,1)} %constant_dynamic-update-slice_fusion, s32[]{:T(128)S(6)} %select_n.29), kind=kOutput, calls=%fused_computation.22 | convolution fusion | flops 4026925056 | bytes 13893636 | tf_op jit(solution)/shard_map/td,ide->ite/dot_general | solution.py:65
  127.9 5.5 %collective-permute-start.3 = (bf16[2,256,256]{2,1,0:T(8,128)(2,1)S(1)}, bf16[2,256,256]{2,1,0:T(8,128)(2,1)S(1)}, u32[]{:S(2)}, u32[]{:S(2)}) collective-permute-start(bf16[2,256,256]{2,1,0:T(8,128)(2,1)S(1)} %get-tuple-element.7), channel_id=1, source_target_pairs={{0,4},{4,8},{8,12},{1,5},{5,9},{9,13},{2,6},{6,10},{10,14},{3,7},{... | collective-permute-start | bytes 786440 | tf_op jit(solution)/shard_map/ppermute | solution.py:19
  133.4 1.9 %collective-permute-start.4 = (bf16[2,256,256]{2,1,0:T(8,128)(2,1)S(1)}, bf16[2,256,256]{2,1,0:T(8,128)(2,1)S(1)}, u32[]{:S(2)}, u32[]{:S(2)}) collective-permute-start(bf16[2,256,256]{2,1,0:T(8,128)(2,1)S(1)} %get-tuple-element.8), channel_id=1, source_target_pairs={{4,0},{8,4},{12,8},{5,1},{9,5},{13,9},{6,2},{10,6},{14,10},{7,3},{... | collective-permute-start | bytes 786440 | tf_op jit(solution)/shard_map/ppermute | solution.py:20
  135.4 0.0 copy-done.4
  135.4 0.1 iota_compare_fusion
  135.5 0.1 reshape_squeeze.10
  135.6 1.1 collective-permute-done.3
  136.7 4.4 %collective-permute-done.4 = bf16[2,256,256]{2,1,0:T(8,128)(2,1)S(1)} collective-permute-done((bf16[2,256,256]{2,1,0:T(8,128)(2,1)S(1)}, bf16[2,256,256]{2,1,0:T(8,128)(2,1)S(1)}, u32[]{:S(2)}, u32[]{:S(2)}) %collective-permute-start.4) | collective-permute-done | bytes 262176 | tf_op jit(solution)/shard_map/ppermute | solution.py:20
  141.1 0.1 pad_maximum_fusion
  141.2 0.1 fusion.34
  141.3 0.1 reshape_squeeze.11
  141.4 0.1 copy.15
  141.5 0.8 gather_fusion.1
  142.3 0.1 copy.17
  142.4 0.5 fusion.29
  142.9 0.4 fusion.9
  143.3 0.6 fusion.10
  143.9 0.9 reshape_squeeze.9
  144.8 1.1 copy.14
  146.0 1.9 %gather_fusion = bf16[20,128,2,128]{3,1,2,0:T(8,128)(2,1)} fusion(bf16[8,128,2,128]{3,1,2,0:T(8,128)(2,1)S(1)} %copy.14, s32[1024]{0:T(1024)S(1)} %pad_clamp_fusion), kind=kCustom, calls=%fused_computation | custom fusion | bytes 2621520 | tf_op jit(solution)/shard_map/gather | solution.py:32
  147.8 2.4 %fusion.26 = bf16[4,128,2,128]{1,3,2,0:T(8,128)(2,1)S(1)} fusion(f32[4,2,128,5,128]{2,4,3,1,0:T(8,128)S(1)} %bitcast.38, f32[4,2,128]{2,1,0:T(2,128)S(1)} %fusion.10, f32[4,2,128]{2,1,0:T(2,128)S(1)} %fusion.9, pred[4,5]{1,0:T(4,128)(4,1)S(1)} %iota_compare_fusion, bf16[4,5,128,2,128]{4,2,3,1,0:T(8,128)(2,1)} %bitcast.41), kind=kOutput, calls=%fused_computation.25 | convolution fusion | flops 171180032 | bytes 4202516 | tf_op jit(solution)/shard_map/phtks,pkshd->pthd/dot_general | solution.py:43
  150.2 0.2 copy.20
  150.4 0.7 copy.37
  (8 shorter events, 0.1 us)
Async XLA Ops:
  6.5 1.3 copy-start
  6.5 2.1 %copy-start.2 = (f32[5120]{0:T(1024)S(1)}, f32[5120]{0:T(1024)}, u32[]{:S(2)}) copy-start(f32[5120]{0:T(1024)} %param.8) | copy-start | bytes 61444
  6.5 2.1 %copy-start.1 = (f32[5120]{0:T(1024)S(1)}, f32[5120]{0:T(1024)}, u32[]{:S(2)}) copy-start(f32[5120]{0:T(1024)} %param.7) | copy-start | bytes 61444
  6.5 112.3 %all-gather.2.cloned.1.call-start = ((), (), s32[]{:S(2)}) async-start(), calls=%async_computation | async-start | bytes 9830400 | tf_op jit(solution)/shard_map/all_gather | solution.py:68
  7.9 65.1 %copy-start.3 = (s32[1,4,5]{2,1,0:T(4,128)S(1)}, s32[1,4,5]{2,1,0:T(4,128)}, u32[]{:S(2)}) copy-start(s32[1,4,5]{2,1,0:T(4,128)} %param.10) | copy-start | bytes 244
  9.3 32.7 %collective-permute-start = (bf16[128,5120]{1,0:T(8,128)(2,1)S(1)}, bf16[128,5120]{1,0:T(8,128)(2,1)S(1)}, u32[]{:S(2)}, u32[]{:S(2)}) collective-permute-start(bf16[128,5120]{1,0:T(8,128)(2,1)S(1)} %fusion.8), channel_id=1, source_target_pairs={{0,1},{1,2},{2,3},{3,0},{4,5},{5,6},{6,7},{7,4},{8,9},{9,10},{10,1... | collective-permute-start | bytes 3932168 | tf_op jit(solution)/shard_map/ppermute | solution.py:61
  41.9 31.0 %collective-permute-start.1 = (bf16[128,5120]{1,0:T(8,128)(2,1)S(1)}, bf16[128,5120]{1,0:T(8,128)(2,1)}, u32[]{:S(2)}, u32[]{:S(2)}) collective-permute-start(bf16[128,5120]{1,0:T(8,128)(2,1)S(1)} %collective-permute-done), channel_id=1, source_target_pairs={{0,1},{1,2},{2,3},{3,0},{4,5},{5,6},{6,7},{7,4},{8,9},{9,10},{10,1... | collective-permute-start | bytes 3932168 | tf_op jit(solution)/shard_map/ppermute | solution.py:61
  72.9 30.3 %collective-permute-start.2 = (bf16[128,5120]{1,0:T(8,128)(2,1)}, bf16[128,5120]{1,0:T(8,128)(2,1)}, u32[]{:S(2)}, u32[]{:S(2)}) collective-permute-start(bf16[128,5120]{1,0:T(8,128)(2,1)} %collective-permute-done.1), channel_id=1, source_target_pairs={{0,1},{1,2},{2,3},{3,0},{4,5},{5,6},{6,7},{7,4},{8,9},{9,10},{10,1... | collective-permute-start | bytes 3932168 | tf_op jit(solution)/shard_map/ppermute | solution.py:61
  118.8 16.6 %copy-start.4 = (s32[1,4]{1,0:T(1,128)S(1)}, s32[1,4]{1,0:T(1,128)}, u32[]{:S(2)}) copy-start(s32[1,4]{1,0:T(1,128)} %param.11) | copy-start | bytes 52
  127.9 8.8 %collective-permute-start.3 = (bf16[2,256,256]{2,1,0:T(8,128)(2,1)S(1)}, bf16[2,256,256]{2,1,0:T(8,128)(2,1)S(1)}, u32[]{:S(2)}, u32[]{:S(2)}) collective-permute-start(bf16[2,256,256]{2,1,0:T(8,128)(2,1)S(1)} %get-tuple-element.7), channel_id=1, source_target_pairs={{0,4},{4,8},{8,12},{1,5},{5,9},{9,13},{2,6},{6,10},{10,14},{3,7},{... | collective-permute-start | bytes 786440 | tf_op jit(solution)/shard_map/ppermute | solution.py:19
  133.4 7.7 %collective-permute-start.4 = (bf16[2,256,256]{2,1,0:T(8,128)(2,1)S(1)}, bf16[2,256,256]{2,1,0:T(8,128)(2,1)S(1)}, u32[]{:S(2)}, u32[]{:S(2)}) collective-permute-start(bf16[2,256,256]{2,1,0:T(8,128)(2,1)S(1)} %get-tuple-element.8), channel_id=1, source_target_pairs={{4,0},{8,4},{12,8},{5,1},{9,5},{13,9},{6,2},{10,6},{14,10},{7,3},{... | collective-permute-start | bytes 786440 | tf_op jit(solution)/shard_map/ppermute | solution.py:20
Sparse Core Ops, SparseCore 0:
  8.9 57.7 all-gather.1
